TPU v7x, 512 devices: a whole 4x8x8 slice. The times are simulated.
512 devices in a mesh: seq: 64 (over z, y_lo, core), head: 8 (over y_hi, x).
Axes of the slice: x: 4, y: 8 (y_hi: 2, y_lo: 4; y = y_hi * 4 + y_lo), z: 8, core: 2. Of those that a mesh axis runs over, the one named last changes fastest.
Arguments:
- query_in: bfloat16 [24576, 2048], P('seq', 'head'), may hold values from -6 to 6
- key_in: bfloat16 [24576, 2048], P('seq', 'head'), may hold values from -6 to 6
- value_in: bfloat16 [24576, 2048], P('seq', 'head'), may hold values from -6 to 6
- text_keys: bfloat16 [256, 2048], P(None, 'head'), may hold values from -6 to 6
- text_values: bfloat16 [256, 2048], P(None, 'head'), may hold values from -6 to 6
- text_mask: int32 [256], replicated, may hold values 0 or 1
- window_reach: int32 [16, 2], P('head'), may hold values from 0 to 1
- tile_map: int32 [64, 3], replicated, may hold values from 0 to 14, as said below
- out_weight: bfloat16 [2048, 3072], P('head'), may hold values from -0.125 to 0.125
- gate_scale: float32 [3072], replicated, may hold values from -4 to 4
- grad_out: bfloat16 [24576, 3072], P('seq', 'head'), may hold values from -12 to 12
Outputs:
- grad_query: bfloat16 [24576, 2048], P('seq', 'head')
- grad_key: bfloat16 [24576, 2048], P('seq', 'head')
- grad_value: bfloat16 [24576, 2048], P('seq', 'head')
- grad_text_keys: bfloat16 [256, 2048], P(None, 'head')
- grad_text_values: bfloat16 [256, 2048], P(None, 'head')
- grad_gate: float32 [3072], replicated
Inputs may be any that keep to these rules, and one draw needn't show every extreme that they name: `tile_map`: index i of seq sits at grid row i // 8 and grid column i % 8. Its tile row is that grid row, or 7 minus it, plus an offset; its tile column is the grid column, or 7 minus it, plus an offset; the mirroring and the offsets are the same for all indices, and so is the frame coordinate. Of the two offsets, the one of the longer grid dimension (rows when they are equal) is 7, the other 0.
All inputs are finite; a program needn't handle non-finite values.
Results may differ from a plain program's by a relative error of at most 0.02035.
The roundings to bfloat16 on the way count: a program that leaves them out, or rounds other values in their place, can miss the bound.
Values may be sent and summed in bfloat16 or wider, within the bound.
No kernel may reach another device: no remote copies, remote signals or barrier semaphores. Data moves between devices by JAX's collectives and lax.ppermute only.
A program may use at most 64 MiB of HBM per device.

v0:
```python
import jax
import jax.numpy as jnp
import numpy as np
from jax import lax
from jax.sharding import PartitionSpec as P

HEAD_DIM = 128
TILE_T = 6
TILE_H = 8
TILE_W = 8
COLS = 8
theta_base = 256.0


def from_behind(array, axis, by):
    length = lax.axis_size(axis)
    pairs = [(i, i + by) for i in range(length) if 0 <= i + by < length]
    return lax.ppermute(array, axis, pairs)


def sections(head_dim):
    first = head_dim // 8
    second = (head_dim - first) // 2
    return ((0, first), (first, second), (first + second, second))


def rotate(values, frame_pos, row_pos, col_pos, direction):
    pieces = []
    for (offset, length), where_pos in zip(
        sections(values.shape[-1]), (frame_pos, row_pos, col_pos)
    ):
        half_len = length // 2
        freqs = theta_base ** (-2.0 * jnp.arange(half_len, dtype=jnp.float32) / length)
        angles = where_pos.astype(jnp.float32)[:, None] * freqs[None, :]
        cosine = jnp.cos(angles)[:, None, :]
        sine_part = jnp.sin(angles)[:, None, :]
        first_half = values[..., offset : offset + half_len]
        second_half = values[..., offset + half_len : offset + length]
        pieces.append(first_half * cosine - direction * second_half * sine_part)
        pieces.append(direction * first_half * sine_part + second_half * cosine)
    return jnp.concatenate(pieces, axis=-1)


def local_positions(tile_coords):
    local_index = jnp.arange(TILE_T * TILE_H * TILE_W, dtype=jnp.int32)
    plane_size = TILE_H * TILE_W
    frame_pos = tile_coords[:, 0:1] * TILE_T + (local_index // plane_size)[None, :]
    row_pos = tile_coords[:, 1:2] * TILE_H + (local_index // TILE_W % TILE_H)[None, :]
    col_pos = tile_coords[:, 2:3] * TILE_W + (local_index % TILE_W)[None, :]
    return (frame_pos.reshape(-1), row_pos.reshape(-1), col_pos.reshape(-1))


def head_scores(queries, key_block, score_scale):
    return (
        jnp.einsum("qhd,khd->hqk", queries, key_block, preferred_element_type=jnp.float32)
        * score_scale
    )


def merge_stats(running_max, running_sum, scores):
    new_max = jnp.maximum(running_max, jnp.max(scores, axis=-1))
    new_sum = running_sum * jnp.exp(running_max - new_max) + jnp.sum(
        jnp.exp(scores - new_max[..., None]), axis=-1
    )
    return (new_max, new_sum)


def on_device(
    query_in,
    key_in,
    value_in,
    text_keys,
    text_values,
    text_mask,
    window_reach,
    tile_map,
    out_weight,
    gate_scale,
    grad_out,
):
    tile_rows = query_in.shape[0]
    feature_width = query_in.shape[1]
    head_count = feature_width // HEAD_DIM
    text_count = text_keys.shape[0]
    row_count = lax.axis_size("seq") // COLS
    device = lax.axis_index("seq")
    score_scale = HEAD_DIM ** (-0.5)
    split_shape = (tile_rows, head_count, HEAD_DIM)
    own_coords = tile_map[device]
    frame_pos, row_pos, col_pos = local_positions(own_coords[None, :])
    queries = rotate(
        query_in.astype(jnp.float32).reshape(split_shape), frame_pos, row_pos, col_pos, 1.0
    ).astype(jnp.bfloat16)
    keys_rot = rotate(
        key_in.astype(jnp.float32).reshape(split_shape), frame_pos, row_pos, col_pos, 1.0
    ).astype(jnp.bfloat16)
    packed = jnp.stack([keys_rot.reshape(tile_rows, feature_width), value_in])
    row_steps = np.array([-1, -1, -1, 0, 0, 0, 1, 1, 1], dtype=np.int32)
    col_steps = np.array([-1, 0, 1, -1, 0, 1, -1, 0, 1], dtype=np.int32)
    fetched = []
    for number in range(9):
        if number == 4:
            fetched.append(packed)
        else:
            fetched.append(
                from_behind(packed, "seq", int(row_steps[number]) * COLS + int(col_steps[number]))
            )
    blocks = jnp.stack(fetched)
    source_row = device // COLS - jnp.asarray(row_steps)
    source_col = device % COLS - jnp.asarray(col_steps)
    usable_block = (
        (source_row >= 0) & (source_row < row_count) & (source_col >= 0) & (source_col < COLS)
    )
    source = jnp.clip(source_row, 0, row_count - 1) * COLS + jnp.clip(source_col, 0, COLS - 1)
    near_coords = tile_map[source]
    row_gap = jnp.abs(near_coords[:, 1] - own_coords[1])
    col_gap = jnp.abs(near_coords[:, 2] - own_coords[2])
    allowed = (
        usable_block[None, :]
        & (row_gap[None, :] <= window_reach[:, 0:1])
        & (col_gap[None, :] <= window_reach[:, 1:2])
    )
    allow_rows = allowed.T
    text_open = (text_mask == 1)[None, None, :]
    block_keys = blocks[:, 0].reshape(9, tile_rows, head_count, HEAD_DIM)
    block_values = blocks[:, 1].reshape(9, tile_rows, head_count, HEAD_DIM)
    text_key_split = text_keys.reshape(text_count, head_count, HEAD_DIM)
    text_value_split = text_values.reshape(text_count, head_count, HEAD_DIM)

    def stats_step(carry, inputs):
        key_block, allow = inputs
        scores = jnp.where(
            allow[:, None, None], head_scores(queries, key_block, score_scale), -jnp.inf
        )
        return (merge_stats(carry[0], carry[1], scores), None)

    start_stats = (
        jnp.full((head_count, tile_rows), -1e30, jnp.float32),
        jnp.zeros((head_count, tile_rows), jnp.float32),
    )
    (running_max, running_sum), _ = lax.scan(stats_step, start_stats, (block_keys, allow_rows))
    text_scores = jnp.where(text_open, head_scores(queries, text_key_split, score_scale), -jnp.inf)
    running_max, running_sum = merge_stats(running_max, running_sum, text_scores)
    log_norm = running_max + jnp.log(running_sum)

    def weights_for(key_block, allow_mask):
        scores = head_scores(queries, key_block, score_scale)
        return jnp.where(allow_mask, jnp.exp(scores - log_norm[:, :, None]), 0.0)

    def output_step(total_out, inputs):
        key_block, value_block, allow = inputs
        probs = weights_for(key_block, allow[:, None, None]).astype(jnp.bfloat16)
        return (
            total_out
            + jnp.einsum("hqk,khd->hqd", probs, value_block, preferred_element_type=jnp.float32),
            None,
        )

    total_out, _ = lax.scan(
        output_step,
        jnp.zeros((head_count, tile_rows, HEAD_DIM), jnp.float32),
        (block_keys, block_values, allow_rows),
    )
    text_probs = weights_for(text_key_split, text_open).astype(jnp.bfloat16)
    total_out = total_out + jnp.einsum(
        "hqk,khd->hqd", text_probs, text_value_split, preferred_element_type=jnp.float32
    )
    attn = total_out.transpose(1, 0, 2).reshape(tile_rows, feature_width).astype(jnp.bfloat16)
    piece = lax.all_gather(grad_out, "head", axis=1, tiled=True)
    grad_proj = (piece.astype(jnp.float32) * gate_scale[None, :]).astype(jnp.bfloat16)
    grad_acc = lax.dot_general(
        grad_proj, out_weight, (((1,), (1,)), ((), ())), preferred_element_type=jnp.float32
    )
    projected = jnp.dot(attn, out_weight, preferred_element_type=jnp.float32)
    terms = jnp.sum(piece.astype(jnp.float32) * projected, axis=0)
    gate_terms = terms
    grad_attn, gate_terms = (grad_acc, gate_terms)
    grad_heads = grad_attn.astype(jnp.bfloat16).reshape(split_shape)
    delta = jnp.sum(
        grad_heads.astype(jnp.float32) * attn.reshape(split_shape).astype(jnp.float32), axis=-1
    ).T

    def grad_block(key_block, value_block, allow_mask):
        weights = weights_for(key_block, allow_mask)
        grad_weights = jnp.einsum(
            "qhd,khd->hqk", grad_heads, value_block, preferred_element_type=jnp.float32
        )
        grad_scores = (weights * (grad_weights - delta[:, :, None])).astype(jnp.bfloat16)
        query_part = jnp.einsum(
            "hqk,khd->hqd", grad_scores, key_block, preferred_element_type=jnp.float32
        )
        key_part = (
            jnp.einsum("hqk,qhd->khd", grad_scores, queries, preferred_element_type=jnp.float32)
            * score_scale
        )
        value_part = jnp.einsum(
            "hqk,qhd->khd",
            weights.astype(jnp.bfloat16),
            grad_heads,
            preferred_element_type=jnp.float32,
        )
        return (query_part, key_part, value_part)

    text_query_part, text_key_part, text_value_part = grad_block(
        text_key_split, text_value_split, text_open
    )
    text_key_grad = text_key_part.reshape(text_count, feature_width)
    text_value_grad = text_value_part.reshape(text_count, feature_width)

    def back_step(query_acc, inputs):
        key_block, value_block, allow = inputs
        query_part, key_part, value_part = grad_block(key_block, value_block, allow[:, None, None])
        stacked = jnp.stack(
            [
                key_part.reshape(tile_rows, feature_width),
                value_part.reshape(tile_rows, feature_width),
            ]
        )
        return (query_acc + query_part, stacked)

    query_acc, partials = lax.scan(
        back_step,
        jnp.zeros((head_count, tile_rows, HEAD_DIM), jnp.float32),
        (block_keys, block_values, allow_rows),
    )
    own_total = partials[4]
    for number in range(9):
        if number != 4:
            own_total = own_total + from_behind(
                partials[number].astype(jnp.bfloat16),
                "seq",
                -(int(row_steps[number]) * COLS + int(col_steps[number])),
            ).astype(jnp.float32)
    query_acc = query_acc + text_query_part
    text_key_sum, text_value_sum = lax.psum((text_key_grad, text_value_grad), "seq")
    grad_gate = lax.psum(gate_terms, ("seq", "head"))
    grad_query = (
        rotate((query_acc * score_scale).transpose(1, 0, 2), frame_pos, row_pos, col_pos, -1.0)
        .astype(jnp.bfloat16)
        .reshape(tile_rows, feature_width)
    )
    grad_key = (
        rotate(own_total[0].reshape(split_shape), frame_pos, row_pos, col_pos, -1.0)
        .astype(jnp.bfloat16)
        .reshape(tile_rows, feature_width)
    )
    grad_value = own_total[1].astype(jnp.bfloat16)
    return (
        grad_query,
        grad_key,
        grad_value,
        text_key_sum.astype(jnp.bfloat16),
        text_value_sum.astype(jnp.bfloat16),
        grad_gate,
    )


def solution(mesh):
    placed = (
        P("seq", "head"),
        P("seq", "head"),
        P("seq", "head"),
        P(None, "head"),
        P(None, "head"),
        P(),
        P("head", None),
        P(),
        P("head", None),
        P(),
        P("seq", "head"),
    )
    return jax.shard_map(
        on_device,
        mesh=mesh,
        in_specs=placed,
        out_specs=(
            P("seq", "head"),
            P("seq", "head"),
            P("seq", "head"),
            P(None, "head"),
            P(None, "head"),
            P(),
        ),
        check_vma=False,
    )
```

profile of v0, /device:TPU:2, one launch (start us, length us, event | category | flops | bytes accessed | tf_op | source)
XLA Modules:
  0.0 668.5 jit_solution(16040238661851726279)
XLA Ops:
  18.0 1.8 copy.175
  25.4 1.7 copy.171
  27.2 2.4 broadcast_multiply_fusion
  29.5 2.1 add_convert_fusion.8
  32.2 2.1 concatenate.16
  36.2 5.0 collective-permute-start.6
  41.2 5.4 collective-permute-start.5
  46.7 2.0 collective-permute-start.4
  55.3 1.7 copy.182
  57.0 1.5 copy.135
  58.5 1.4 concatenate.17
  60.1 1.4 gather_fusion
  61.6 1.8 select_reduce_fusion
  66.2 3.7 collective-permute-done
  74.5 15.0 %collective-permute-done.2 = bf16[2,384,256]{1,2,0:T(8,128)(2,1)S(1)} collective-permute-done((bf16[2,384,256]{1,2,0:T(8,128)(2,1)}, bf16[2,384,256]{1,2,0:T(8,128)(2,1)S(1)}, u32[]{:S(2)}, u32[]{:S(2)}) %collective-permute-start.2) | collective-permute-done | bytes 393248 | tf_op jit(solution)/shard_map/ppermute | solution.py:18
  89.5 1.5 collective-permute-start.7
  94.5 1.9 collective-permute-done.7
  96.5 2.3 fusion.93
  98.8 3.8 copy.126
  102.6 13.8 %while.37 = (s32[]{:T(128)}, f32[2,384]{1,0:T(2,128)S(1)}, f32[2,384]{1,0:T(2,128)S(1)}, pred[9,2]{1,0:T(8,128)(4,1)S(1)}, bf16[9,384,2,128]{3,1,2,0:T(8,128)(2,...) while((s32[]{:T(128)}, f32[2,384]{1,0:T(2,128)S(1)}, f32[2,384]{1,0:T(2,128)S(1)}, ...), condition=%wide.region_3.4_spmd.clone, body=%wide.region_0.3_spmd.clone.sunk | while | flops 76975872 | bytes 2792566 | solution.py:141
  117.0 3.9 copy.128
  121.2 29.6 %while.38 = (s32[]{:T(128)}, f32[2,384,128]{2,1,0:T(8,128)}, pred[9,2]{1,0:T(8,128)(4,1)}, bf16[9,384,2,128]{3,1,2,0:T(8,128)(2,1)}, bf16[384,2,128]{2,0,1:T(8,1...) while((s32[]{:T(128)}, f32[2,384,128]{2,1,0:T(8,128)}, ...), condition=%wide.region_7.8_spmd.clone, body=%wide.region_6.7_spmd.clone.sunk | while | flops 152371200 | bytes 1380984 | solution.py:159
  121.9 2.4 fusion.151
  125.0 2.6 fusion.151
  128.3 2.6 fusion.151
  131.6 2.6 fusion.151
  134.9 2.6 fusion.151
  138.2 2.6 fusion.151
  141.5 2.6 fusion.151
  144.8 2.6 fusion.151
  148.1 2.6 fusion.151
  150.8 1.9 copy.125
  152.7 2.7 fusion.53
  158.5 55.7 %while.39 = (s32[]{:T(128)}, f32[2,384,128]{2,1,0:T(8,128)S(1)}, f32[9,2,384,256]{2,3,1,0:T(8,128)}, pred[9,2]{1,0:T(8,128)(4,1)}, bf16[9,384,2,128]{3,1,2,0:T(8...) while((s32[]{:T(128)}, f32[2,384,128]{2,1,0:T(8,128)S(1)}, ...), condition=%wide.region_10.11_spmd.clone, body=%wide.region_9.10_spmd.clone.sunk | while | flops 380043264 | bytes 9836705 | solution.py:221
  162.0 1.4 convolution_add_fusion.4
  214.2 3.6 convert.109
  217.7 1.8 slice_bitcast_fusion.7
  219.5 5.7 collective-permute-start.8
  229.9 1.8 copy.146
  234.3 2.5 fusion.45
  236.9 126.0 %psum.23 = f32[3072]{0:T(1024)} all-reduce(f32[3072]{0:T(1024)S(1)} %fusion.45), channel_id=1, replica_groups=mesh['seq'=64,'head'=8] {'seq','head'}, use_global_device_ids=true, to_apply=%region_14.15 | all-reduce | flops 3072 | bytes 24576 | tf_op jit(solution)/shard_map/psum | solution.py:236
  362.9 2.5 collective-permute-start.11
  365.4 7.6 %collective-permute-start.10 = (bf16[2,384,256]{1,2,0:T(8,128)(2,1)}, bf16[2,384,256]{1,2,0:T(8,128)(2,1)}, u32[]{:S(2)}, u32[]{:S(2)}) collective-permute-start(bf16[2,384,256]{1,2,0:T(8,128)(2,1)} %get-tuple-element.347), channel_id=1, source_target_pairs={{0,56},{8,64},{16,72},{24,80},{32,88},{40,96},{48,104},{56,112},{6... | collective-permute-start | bytes 1179656 | tf_op jit(solution)/shard_map/ppermute | solution.py:18
  373.0 2.4 collective-permute-start.9
  375.7 269.2 %all-reduce.2 = (bf16[256,256]{1,0:T(8,128)(2,1)}, bf16[256,256]{1,0:T(8,128)(2,1)}) all-reduce(f32[256,256]{1,0:T(8,128)} %copy.146, f32[256,256]{1,0:T(8,128)S(1)} %copy.148), channel_id=1, replica_groups=mesh['seq'=64,'head'=8] {'seq'}, use_global_device_ids=true, to_apply=%region_11.12 | all-reduce | flops 131072 | bytes 786432 | tf_op jit(solution)/shard_map/psum | solution.py:235
  644.9 2.5 fusion.63
  653.8 2.2 add_convert_fusion.2
  657.4 1.6 concatenate.18
  (296 shorter events, 130.0 us)
Async XLA Ops:
  7.2 145.5 %copy-start = (bf16[256,3072]{1,0:T(8,128)(2,1)S(1)}, bf16[256,3072]{1,0:T(8,128)(2,1)}, u32[]{:S(2)}) copy-start(bf16[256,3072]{1,0:T(8,128)(2,1)} %param.27) | copy-start | bytes 4718596
  7.2 4.3 copy-start.31
  7.2 7.7 %copy-start.28 = (bf16[384,256]{1,0:T(8,128)(2,1)S(1)}, bf16[384,256]{1,0:T(8,128)(2,1)}, u32[]{:S(2)}) copy-start(bf16[384,256]{1,0:T(8,128)(2,1)} %param.21) | copy-start | bytes 589828
  7.2 145.5 %all-gather.2.cloned.1.call-start = ((), (), s32[]{:S(2)}) async-start(), calls=%async_computation | async-start | bytes 2654208 | tf_op jit(solution)/shard_map/all_gather | solution.py:169
  14.8 14.8 %copy-start.6 = (f32[384,8]{1,0:T(8,128)}, f32[384,8]{1,0:T(8,128)S(1)}, u32[]{:S(2)}) copy-start(f32[384,8]{1,0:T(8,128)S(1)} %copy.103) | copy-start | bytes 36868
  27.1 4.5 copy-start.9
  27.1 4.5 copy-start.10
  27.1 4.5 copy-start.11
  27.1 4.5 copy-start.12
  27.1 4.5 copy-start.13
  27.1 4.5 copy-start.14
  27.1 4.5 copy-start.15
  27.1 4.5 copy-start.16
  29.5 2.7 copy-start.2
  32.2 21.0 %copy-start.32 = (s32[2,2]{1,0:T(2,128)S(1)}, s32[2,2]{1,0:T(2,128)}, u32[]{:S(2)}) copy-start(s32[2,2]{1,0:T(2,128)} %param.25) | copy-start | bytes 52
  35.4 23.1 %copy-start.4 = (bf16[384,2,128]{0,2,1:T(8,128)(2,1)}, bf16[384,2,128]{0,2,1:T(8,128)(2,1)S(1)}, u32[]{:S(2)}) copy-start(bf16[384,2,128]{0,2,1:T(8,128)(2,1)S(1)} %copy.110) | copy-start | bytes 589828
  36.2 57.2 %collective-permute-start.6 = (bf16[2,384,256]{1,2,0:T(8,128)(2,1)}, bf16[2,384,256]{1,2,0:T(8,128)(2,1)}, u32[]{:S(2)}, u32[]{:S(2)}) collective-permute-start(bf16[2,384,256]{1,2,0:T(8,128)(2,1)} %pad_maximum_fusion), channel_id=1, source_target_pairs={{0,64},{8,72},{16,80},{24,88},{32,96},{40,104},{48,112},{56,120},{... | collective-permute-start | bytes 1179656 | tf_op jit(solution)/shard_map/ppermute | solution.py:18
  41.2 51.1 %collective-permute-start.5 = (bf16[2,384,256]{1,2,0:T(8,128)(2,1)}, bf16[2,384,256]{1,2,0:T(8,128)(2,1)}, u32[]{:S(2)}, u32[]{:S(2)}) collective-permute-start(bf16[2,384,256]{1,2,0:T(8,128)(2,1)} %pad_maximum_fusion), channel_id=1, source_target_pairs={{0,56},{8,64},{16,72},{24,80},{32,88},{40,96},{48,104},{56,112},{6... | collective-permute-start | bytes 1179656 | tf_op jit(solution)/shard_map/ppermute | solution.py:18
  46.7 44.6 %collective-permute-start.4 = (bf16[2,384,256]{1,2,0:T(8,128)(2,1)}, bf16[2,384,256]{1,2,0:T(8,128)(2,1)}, u32[]{:S(2)}, u32[]{:S(2)}) collective-permute-start(bf16[2,384,256]{1,2,0:T(8,128)(2,1)} %pad_maximum_fusion), channel_id=1, source_target_pairs={{0,8},{8,16},{16,24},{24,32},{32,40},{40,48},{48,56},{56,64},{64,7... | collective-permute-start | bytes 1179656 | tf_op jit(solution)/shard_map/ppermute | solution.py:18
  48.7 23.5 %collective-permute-start.1 = (bf16[2,384,256]{1,2,0:T(8,128)(2,1)}, bf16[2,384,256]{1,2,0:T(8,128)(2,1)}, u32[]{:S(2)}, u32[]{:S(2)}) collective-permute-start(bf16[2,384,256]{1,2,0:T(8,128)(2,1)} %pad_maximum_fusion), channel_id=1, source_target_pairs={{64,0},{72,8},{80,16},{88,24},{96,32},{104,40},{112,48},{120,56},{... | collective-permute-start | bytes 1179656 | tf_op jit(solution)/shard_map/ppermute | solution.py:18
  50.0 19.8 %collective-permute-start = (bf16[2,384,256]{1,2,0:T(8,128)(2,1)}, bf16[2,384,256]{1,2,0:T(8,128)(2,1)}, u32[]{:S(2)}, u32[]{:S(2)}) collective-permute-start(bf16[2,384,256]{1,2,0:T(8,128)(2,1)} %pad_maximum_fusion), channel_id=1, source_target_pairs={{72,0},{80,8},{88,16},{96,24},{104,32},{112,40},{120,48},{128,56},... | collective-permute-start | bytes 1179656 | tf_op jit(solution)/shard_map/ppermute | solution.py:18
  63.4 27.8 %copy-start.5 = (bf16[384,2,128]{0,2,1:T(8,128)(2,1)S(1)}, bf16[384,2,128]{0,2,1:T(8,128)(2,1)}, u32[]{:S(2)}) copy-start(bf16[384,2,128]{0,2,1:T(8,128)(2,1)} %copy-done.4) | copy-start | bytes 589828
  69.8 19.7 %collective-permute-start.2 = (bf16[2,384,256]{1,2,0:T(8,128)(2,1)}, bf16[2,384,256]{1,2,0:T(8,128)(2,1)S(1)}, u32[]{:S(2)}, u32[]{:S(2)}) collective-permute-start(bf16[2,384,256]{1,2,0:T(8,128)(2,1)} %pad_maximum_fusion), channel_id=1, source_target_pairs={{56,0},{64,8},{72,16},{80,24},{88,32},{96,40},{104,48},{112,56},{1... | collective-permute-start | bytes 1179656 | tf_op jit(solution)/shard_map/ppermute | solution.py:18
  72.2 19.0 %collective-permute-start.3 = (bf16[2,384,256]{1,2,0:T(8,128)(2,1)}, bf16[2,384,256]{1,2,0:T(8,128)(2,1)S(1)}, u32[]{:S(2)}, u32[]{:S(2)}) collective-permute-start(bf16[2,384,256]{1,2,0:T(8,128)(2,1)} %pad_maximum_fusion), channel_id=1, source_target_pairs={{8,0},{16,8},{24,16},{32,24},{40,32},{48,40},{56,48},{64,56},{72,6... | collective-permute-start | bytes 1179656 | tf_op jit(solution)/shard_map/ppermute | solution.py:18
  89.5 6.9 %collective-permute-start.7 = (bf16[2,384,256]{1,2,0:T(8,128)(2,1)}, bf16[2,384,256]{1,2,0:T(8,128)(2,1)S(1)}, u32[]{:S(2)}, u32[]{:S(2)}) collective-permute-start(bf16[2,384,256]{1,2,0:T(8,128)(2,1)} %pad_maximum_fusion), channel_id=1, source_target_pairs={{0,72},{8,80},{16,88},{24,96},{32,104},{40,112},{48,120},{56,128},... | collective-permute-start | bytes 1179656 | tf_op jit(solution)/shard_map/ppermute | solution.py:18
  117.0 3.9 copy-start.30
  117.0 3.9 copy-start.29
  152.7 3.8 copy-start.8
  152.7 3.8 copy-start.26
  217.7 10.1 %copy-start.1 = (bf16[2,384,256]{1,2,0:T(8,128)(2,1)S(1)}, bf16[2,384,256]{1,2,0:T(8,128)(2,1)}, u32[]{:S(2)}) copy-start(bf16[2,384,256]{1,2,0:T(8,128)(2,1)} %fusion.50) | copy-start | bytes 1179652
  219.5 14.8 %copy-start.27 = (bf16[2,384,128]{1,2,0:T(8,128)(2,1)S(1)}, bf16[2,384,128]{1,2,0:T(8,128)(2,1)}, u32[]{:S(2)}) copy-start(bf16[2,384,128]{1,2,0:T(8,128)(2,1)} %get-tuple-element.425) | copy-start | bytes 589828
  219.5 143.4 %collective-permute-start.8 = (bf16[2,384,256]{1,2,0:T(8,128)(2,1)}, bf16[2,384,256]{1,2,0:T(8,128)(2,1)}, u32[]{:S(2)}, u32[]{:S(2)}) collective-permute-start(bf16[2,384,256]{1,2,0:T(8,128)(2,1)} %get-tuple-element.341), channel_id=1, source_target_pairs={{0,72},{8,80},{16,88},{24,96},{32,104},{40,112},{48,120},{56,128},... | collective-permute-start | bytes 1179656 | tf_op jit(solution)/shard_map/ppermute | solution.py:18
  225.3 140.1 %collective-permute-start.15 = (bf16[2,384,256]{1,2,0:T(8,128)(2,1)}, bf16[2,384,256]{1,2,0:T(8,128)(2,1)}, u32[]{:S(2)}, u32[]{:S(2)}) collective-permute-start(bf16[2,384,256]{1,2,0:T(8,128)(2,1)} %get-tuple-element.342), channel_id=1, source_target_pairs={{72,0},{80,8},{88,16},{96,24},{104,32},{112,40},{120,48},{128,56},... | collective-permute-start | bytes 1179656 | tf_op jit(solution)/shard_map/ppermute | solution.py:18
  226.5 146.4 %collective-permute-start.14 = (bf16[2,384,256]{1,2,0:T(8,128)(2,1)}, bf16[2,384,256]{1,2,0:T(8,128)(2,1)}, u32[]{:S(2)}, u32[]{:S(2)}) collective-permute-start(bf16[2,384,256]{1,2,0:T(8,128)(2,1)} %get-tuple-element.343), channel_id=1, source_target_pairs={{64,0},{72,8},{80,16},{88,24},{96,32},{104,40},{112,48},{120,56},{... | collective-permute-start | bytes 1179656 | tf_op jit(solution)/shard_map/ppermute | solution.py:18
  231.7 413.2 %collective-permute-start.13 = (bf16[2,384,256]{1,2,0:T(8,128)(2,1)}, bf16[2,384,256]{1,2,0:T(8,128)(2,1)}, u32[]{:S(2)}, u32[]{:S(2)}) collective-permute-start(bf16[2,384,256]{1,2,0:T(8,128)(2,1)} %get-tuple-element.344), channel_id=1, source_target_pairs={{56,0},{64,8},{72,16},{80,24},{88,32},{96,40},{104,48},{112,56},{1... | collective-permute-start | bytes 1179656 | tf_op jit(solution)/shard_map/ppermute | solution.py:18
  233.0 411.9 %collective-permute-start.12 = (bf16[2,384,256]{1,2,0:T(8,128)(2,1)}, bf16[2,384,256]{1,2,0:T(8,128)(2,1)}, u32[]{:S(2)}, u32[]{:S(2)}) collective-permute-start(bf16[2,384,256]{1,2,0:T(8,128)(2,1)} %get-tuple-element.345), channel_id=1, source_target_pairs={{8,0},{16,8},{24,16},{32,24},{40,32},{48,40},{56,48},{64,56},{72,6... | collective-permute-start | bytes 1179656 | tf_op jit(solution)/shard_map/ppermute | solution.py:18
  234.3 141.0 %copy-start.21 = (bf16[256,256]{0,1:T(8,128)(2,1)S(1)}, bf16[256,256]{0,1:T(8,128)(2,1)}, u32[]{:S(2)}) copy-start(bf16[256,256]{0,1:T(8,128)(2,1)} %copy.182) | copy-start | bytes 393220
  362.9 282.0 %collective-permute-start.11 = (bf16[2,384,256]{1,2,0:T(8,128)(2,1)}, bf16[2,384,256]{1,2,0:T(8,128)(2,1)}, u32[]{:S(2)}, u32[]{:S(2)}) collective-permute-start(bf16[2,384,256]{1,2,0:T(8,128)(2,1)} %get-tuple-element.346), channel_id=1, source_target_pairs={{0,8},{8,16},{16,24},{24,32},{32,40},{40,48},{48,56},{56,64},{64,7... | collective-permute-start | bytes 1179656 | tf_op jit(solution)/shard_map/ppermute | solution.py:18
  365.4 279.6 %collective-permute-start.10 = (bf16[2,384,256]{1,2,0:T(8,128)(2,1)}, bf16[2,384,256]{1,2,0:T(8,128)(2,1)}, u32[]{:S(2)}, u32[]{:S(2)}) collective-permute-start(bf16[2,384,256]{1,2,0:T(8,128)(2,1)} %get-tuple-element.347), channel_id=1, source_target_pairs={{0,56},{8,64},{16,72},{24,80},{32,88},{40,96},{48,104},{56,112},{6... | collective-permute-start | bytes 1179656 | tf_op jit(solution)/shard_map/ppermute | solution.py:18
  373.0 272.0 %collective-permute-start.9 = (bf16[2,384,256]{1,2,0:T(8,128)(2,1)}, bf16[2,384,256]{1,2,0:T(8,128)(2,1)}, u32[]{:S(2)}, u32[]{:S(2)}) collective-permute-start(bf16[2,384,256]{1,2,0:T(8,128)(2,1)} %get-tuple-element.348), channel_id=1, source_target_pairs={{0,64},{8,72},{16,80},{24,88},{32,96},{40,104},{48,112},{56,120},{... | collective-permute-start | bytes 1179656 | tf_op jit(solution)/shard_map/ppermute | solution.py:18
  648.2 5.6 copy-start.7
  652.0 4.1 copy-start.3
  652.0 4.1 copy-start.22
  653.8 2.2 copy-start.17
  653.8 2.2 copy-start.18
  653.8 2.2 copy-start.19
  657.4 2.6 copy-start.24
  657.4 2.6 copy-start.25
  (3 other events, 5.0 us)
Sparse Core Ops, SparseCore 0:
  51.4 93.9 all-gather.1
where the time goes:
time: 672 us; the launch traced here: 668 us
  blocking collectives  395 us (59%)
  matrix products  86.9 us (13%)
  local copies, waits for them, and re-layouts  73.9 us (11%)
  starting transfers between devices  42.5 us (6%)
  other arithmetic  32 us (5%)
  waiting for transfers between devices  20.7 us (3%)
  between operations  16.5 us (2%)
    psum x1, blocking collectives, on_device(): lax.psum((text_key_grad, text_value_grad), 'seq')  269 us
    psum x1, blocking collectives, on_device(): grad_gate = lax.psum(gate_terms, ('seq', 'head'))  126 us
    ppermute x16, starting transfers between devices, from_behind(): return lax.ppermute(array, axis, pairs)  42.4 us
    unnamed x103, local copies, waits for them, and re-layouts  36.4 us
    dot_general x19, matrix products, head_scores(): jnp.einsum('qhd,khd->hqk', queries, key_block, preferred_element_type=jnp...  24.8 us
    dot_general x9, matrix products, output_step(): jnp.einsum('hqk,khd->hqd', probs, value_block, preferred_element_type=jnp...  23.4 us
    ppermute x16, waiting for transfers between devices, from_behind(): return lax.ppermute(array, axis, pairs)  20.7 us
  transfers between devices with their start and end apart: 17, of which 3 were waited for; matrix products, arithmetic and copies ran while one was open for 12% of the time, Pallas kernels for 0%

commit v1 on v0

--- a/solution.py
+++ b/solution.py
@@ -233,7 +233,7 @@
             ).astype(jnp.float32)
     query_acc = query_acc + text_query_part
     text_key_sum, text_value_sum = lax.psum((text_key_grad, text_value_grad), "seq")
-    grad_gate = lax.psum(gate_terms, ("seq", "head"))
+    grad_gate = jnp.sum(lax.all_gather(gate_terms, ("seq", "head")), axis=0)
     grad_query = (
         rotate((query_acc * score_scale).transpose(1, 0, 2), frame_pos, row_pos, col_pos, -1.0)
         .astype(jnp.bfloat16)

time: 672 us -> 1630 us (2.43)
  the two profiles are of different devices: /device:TPU:2 before, /device:TPU:193 now
where the time goes in v1:
time: 1630 us
  waiting for transfers between devices  1080 us (66%)
  blocking collectives  266 us (16%)
  matrix products  82.9 us (5%)
  local copies, waits for them, and re-layouts  77.7 us (5%)
  starting transfers between devices  70.4 us (4%)
  other arithmetic  35.4 us (2%)
  between operations  16.8 us (1%)
    all_gather x1, waiting for transfers between devices, on_device(): grad_gate = jnp.sum(lax.all_gather(gate_terms, ('seq', 'head')), axis=0)  1070 us
    psum x1, blocking collectives, on_device(): lax.psum((text_key_grad, text_value_grad), 'seq')  266 us
    ppermute x16, starting transfers between devices, from_behind(): return lax.ppermute(array, axis, pairs)  70.3 us
    unnamed x99, local copies, waits for them, and re-layouts  34.3 us
  transfers between devices with their start and end apart: 18, of which 4 were waited for; matrix products, arithmetic and copies ran while one was open for 9% of the time, Pallas kernels for 0%

profile of v1, /device:TPU:193, one launch (start us, length us, event | category | flops | bytes accessed | tf_op | source)
XLA Modules:
  0.0 1627.7 jit_solution(7356952836391466720)
XLA Ops:
  18.3 1.8 copy.281
  27.4 2.4 broadcast_multiply_fusion
  29.8 2.1 add_convert_fusion.8
  32.5 2.1 concatenate.16
  36.4 5.2 collective-permute-start.6
  41.6 3.9 collective-permute-start.5
  45.6 2.5 collective-permute-start.4
  48.1 2.2 collective-permute-start.1
  50.3 1.9 collective-permute-start
  56.2 1.7 copy.288
  62.5 1.8 select_reduce_fusion
  68.0 5.4 collective-permute-start.2
  74.4 2.0 collective-permute-start.3
  77.5 7.4 collective-permute-done.2
  84.8 5.8 collective-permute-start.7
  95.6 2.3 fusion.93
  97.9 3.9 copy.232
  101.8 13.8 while.37
  116.2 3.9 copy.234
  120.3 29.4 %while.38 = (s32[]{:T(128)}, f32[2,384,128]{2,1,0:T(8,128)}, pred[9,2]{1,0:T(8,128)(4,1)}, bf16[9,384,2,128]{3,1,2,0:T(8,128)(2,1)}, bf16[384,2,128]{2,0,1:T(8,1...) while((s32[]{:T(128)}, f32[2,384,128]{2,1,0:T(8,128)}, ...), condition=%wide.region_7.8_spmd.clone, body=%wide.region_6.7_spmd.clone.sunk | while | flops 152371200 | bytes 1380984 | solution.py:159
  121.0 2.4 fusion.151
  124.1 2.6 fusion.151
  127.4 2.6 fusion.151
  130.7 2.6 fusion.151
  134.0 2.6 fusion.151
  137.2 2.6 fusion.151
  140.5 2.6 fusion.151
  143.8 2.6 fusion.151
  147.1 2.6 fusion.151
  149.7 1.9 copy.231
  151.6 2.8 fusion.53
  157.5 55.7 %while.39 = (s32[]{:T(128)}, f32[2,384,128]{2,1,0:T(8,128)S(1)}, f32[9,2,384,256]{2,3,1,0:T(8,128)}, pred[9,2]{1,0:T(8,128)(4,1)}, bf16[9,384,2,128]{3,1,2,0:T(8...) while((s32[]{:T(128)}, f32[2,384,128]{2,1,0:T(8,128)S(1)}, ...), condition=%wide.region_10.11_spmd.clone, body=%wide.region_9.10_spmd.clone.sunk | while | flops 380043264 | bytes 9836705 | solution.py:221
  213.1 3.6 convert.109
  216.7 1.7 slice_bitcast_fusion.7
  218.4 6.7 collective-permute-start.8
  225.1 4.7 collective-permute-start.15
  229.8 2.1 collective-permute-start.14
  232.6 3.7 collective-permute-start.13
  236.3 9.9 collective-permute-start.12
  246.2 1.9 collective-permute-start.11
  248.1 7.7 collective-permute-start.10
  255.9 4.7 collective-permute-start.9
  260.9 265.6 %all-reduce.2 = (bf16[256,256]{1,0:T(8,128)(2,1)}, bf16[256,256]{1,0:T(8,128)(2,1)}) all-reduce(f32[256,256]{1,0:T(8,128)S(1)} %copy.252, f32[256,256]{1,0:T(8,128)S(1)} %copy-done.18), channel_id=1, replica_groups=mesh['seq'=64,'head'=8] {'seq'}, use_global_device_ids=true, to_apply=%region_11.12 | all-reduce | flops 131072 | bytes 786432 | tf_op jit(solution)/shard_map/psum | solution.py:235
  526.5 2.2 fusion.63
  533.6 2.1 add_convert_fusion.2
  541.3 1068.5 %all-gather.6.cloned.1.call-done = f32[1572864]{0:T(1024)} async-done(((f32[3072]{0:T(1024)}), f32[1572864]{0:T(1024)}) %all-gather.6.cloned.1.call-update) | async-done | bytes 6291472 | tf_op jit(solution)/shard_map/all_gather | solution.py:236
  1609.8 7.3 reshape.349
  1617.2 3.7 reduce_sum.48
  (296 shorter events, 128.1 us)
Async XLA Ops:
  7.2 144.4 %copy-start = (bf16[256,3072]{1,0:T(8,128)(2,1)S(1)}, bf16[256,3072]{1,0:T(8,128)(2,1)}, u32[]{:S(2)}) copy-start(bf16[256,3072]{1,0:T(8,128)(2,1)} %param.27) | copy-start | bytes 4718596
  7.2 4.3 copy-start.28
  7.2 7.9 copy-start.25
  7.2 144.4 %all-gather.4.cloned.1.call-start = ((), (), s32[]{:S(2)}) async-start(), calls=%async_computation | async-start | bytes 2654208 | tf_op jit(solution)/shard_map/all_gather | solution.py:169
  15.0 14.8 copy-start.6
  27.3 4.5 copy-start.9
  27.3 4.5 copy-start.10
  27.3 4.5 copy-start.11
  27.3 4.5 copy-start.12
  27.3 4.5 copy-start.13
  27.3 4.5 copy-start.14
  27.4 4.5 copy-start.15
  27.4 4.5 copy-start.16
  29.8 2.7 copy-start.2
  32.5 21.8 %copy-start.29 = (s32[2,2]{1,0:T(2,128)S(1)}, s32[2,2]{1,0:T(2,128)}, u32[]{:S(2)}) copy-start(s32[2,2]{1,0:T(2,128)} %param.25) | copy-start | bytes 52
  35.6 23.8 %copy-start.4 = (bf16[384,2,128]{0,2,1:T(8,128)(2,1)}, bf16[384,2,128]{0,2,1:T(8,128)(2,1)S(1)}, u32[]{:S(2)}) copy-start(bf16[384,2,128]{0,2,1:T(8,128)(2,1)S(1)} %copy.216) | copy-start | bytes 589828
  36.4 56.6 %collective-permute-start.6 = (bf16[2,384,256]{1,2,0:T(8,128)(2,1)}, bf16[2,384,256]{1,2,0:T(8,128)(2,1)}, u32[]{:S(2)}, u32[]{:S(2)}) collective-permute-start(bf16[2,384,256]{1,2,0:T(8,128)(2,1)} %pad_maximum_fusion), channel_id=1, source_target_pairs={{0,64},{8,72},{16,80},{24,88},{32,96},{40,104},{48,112},{56,120},{... | collective-permute-start | bytes 1179656 | tf_op jit(solution)/shard_map/ppermute | solution.py:18
  41.6 50.3 %collective-permute-start.5 = (bf16[2,384,256]{1,2,0:T(8,128)(2,1)}, bf16[2,384,256]{1,2,0:T(8,128)(2,1)}, u32[]{:S(2)}, u32[]{:S(2)}) collective-permute-start(bf16[2,384,256]{1,2,0:T(8,128)(2,1)} %pad_maximum_fusion), channel_id=1, source_target_pairs={{0,56},{8,64},{16,72},{24,80},{32,88},{40,96},{48,104},{56,112},{6... | collective-permute-start | bytes 1179656 | tf_op jit(solution)/shard_map/ppermute | solution.py:18
  45.6 45.3 %collective-permute-start.4 = (bf16[2,384,256]{1,2,0:T(8,128)(2,1)}, bf16[2,384,256]{1,2,0:T(8,128)(2,1)}, u32[]{:S(2)}, u32[]{:S(2)}) collective-permute-start(bf16[2,384,256]{1,2,0:T(8,128)(2,1)} %pad_maximum_fusion), channel_id=1, source_target_pairs={{0,8},{8,16},{16,24},{24,32},{32,40},{40,48},{48,56},{56,64},{64,7... | collective-permute-start | bytes 1179656 | tf_op jit(solution)/shard_map/ppermute | solution.py:18
  48.1 26.3 %collective-permute-start.1 = (bf16[2,384,256]{1,2,0:T(8,128)(2,1)}, bf16[2,384,256]{1,2,0:T(8,128)(2,1)}, u32[]{:S(2)}, u32[]{:S(2)}) collective-permute-start(bf16[2,384,256]{1,2,0:T(8,128)(2,1)} %pad_maximum_fusion), channel_id=1, source_target_pairs={{64,0},{72,8},{80,16},{88,24},{96,32},{104,40},{112,48},{120,56},{... | collective-permute-start | bytes 1179656 | tf_op jit(solution)/shard_map/ppermute | solution.py:18
  50.3 17.7 %collective-permute-start = (bf16[2,384,256]{1,2,0:T(8,128)(2,1)}, bf16[2,384,256]{1,2,0:T(8,128)(2,1)}, u32[]{:S(2)}, u32[]{:S(2)}) collective-permute-start(bf16[2,384,256]{1,2,0:T(8,128)(2,1)} %pad_maximum_fusion), channel_id=1, source_target_pairs={{72,0},{80,8},{88,16},{96,24},{104,32},{112,40},{120,48},{128,56},... | collective-permute-start | bytes 1179656 | tf_op jit(solution)/shard_map/ppermute | solution.py:18
  52.3 1557.6 %all-gather.6.cloned.1.call-start = ((), (), s32[]{:S(2)}) async-start(), calls=%async_computation.1 | async-start | bytes 6303744 | tf_op jit(solution)/shard_map/all_gather | solution.py:236
  64.3 26.5 %copy-start.5 = (bf16[384,2,128]{0,2,1:T(8,128)(2,1)S(1)}, bf16[384,2,128]{0,2,1:T(8,128)(2,1)}, u32[]{:S(2)}) copy-start(bf16[384,2,128]{0,2,1:T(8,128)(2,1)} %copy-done.4) | copy-start | bytes 589828
  68.0 16.8 %collective-permute-start.2 = (bf16[2,384,256]{1,2,0:T(8,128)(2,1)}, bf16[2,384,256]{1,2,0:T(8,128)(2,1)S(1)}, u32[]{:S(2)}, u32[]{:S(2)}) collective-permute-start(bf16[2,384,256]{1,2,0:T(8,128)(2,1)} %pad_maximum_fusion), channel_id=1, source_target_pairs={{56,0},{64,8},{72,16},{80,24},{88,32},{96,40},{104,48},{112,56},{1... | collective-permute-start | bytes 1179656 | tf_op jit(solution)/shard_map/ppermute | solution.py:18
  74.4 16.3 %collective-permute-start.3 = (bf16[2,384,256]{1,2,0:T(8,128)(2,1)}, bf16[2,384,256]{1,2,0:T(8,128)(2,1)S(1)}, u32[]{:S(2)}, u32[]{:S(2)}) collective-permute-start(bf16[2,384,256]{1,2,0:T(8,128)(2,1)} %pad_maximum_fusion), channel_id=1, source_target_pairs={{8,0},{16,8},{24,16},{32,24},{40,32},{48,40},{56,48},{64,56},{72,6... | collective-permute-start | bytes 1179656 | tf_op jit(solution)/shard_map/ppermute | solution.py:18
  84.8 10.7 collective-permute-start.7
  116.2 3.9 copy-start.27
  116.2 3.9 copy-start.26
  151.6 2.8 copy-start.8
  151.6 2.9 copy-start.23
  151.6 3.2 copy-start.31
  216.7 15.2 copy-start.24
  218.4 42.2 %copy-start.17 = (bf16[256,256]{0,1:T(8,128)(2,1)S(1)}, bf16[256,256]{0,1:T(8,128)(2,1)}, u32[]{:S(2)}) copy-start(bf16[256,256]{0,1:T(8,128)(2,1)} %copy.288) | copy-start | bytes 393220
  218.4 27.8 %collective-permute-start.8 = (bf16[2,384,256]{1,2,0:T(8,128)(2,1)}, bf16[2,384,256]{1,2,0:T(8,128)(2,1)}, u32[]{:S(2)}, u32[]{:S(2)}) collective-permute-start(bf16[2,384,256]{1,2,0:T(8,128)(2,1)} %get-tuple-element.399), channel_id=1, source_target_pairs={{0,72},{8,80},{16,88},{24,96},{32,104},{40,112},{48,120},{56,128},... | collective-permute-start | bytes 1179656 | tf_op jit(solution)/shard_map/ppermute | solution.py:18
  225.1 23.0 %collective-permute-start.15 = (bf16[2,384,256]{1,2,0:T(8,128)(2,1)}, bf16[2,384,256]{1,2,0:T(8,128)(2,1)}, u32[]{:S(2)}, u32[]{:S(2)}) collective-permute-start(bf16[2,384,256]{1,2,0:T(8,128)(2,1)} %get-tuple-element.400), channel_id=1, source_target_pairs={{72,0},{80,8},{88,16},{96,24},{104,32},{112,40},{120,48},{128,56},... | collective-permute-start | bytes 1179656 | tf_op jit(solution)/shard_map/ppermute | solution.py:18
  229.8 31.1 %copy-start.18 = (f32[256,256]{1,0:T(8,128)S(1)}, f32[256,256]{1,0:T(8,128)}, u32[]{:S(2)}) copy-start(f32[256,256]{1,0:T(8,128)} %copy.254) | copy-start | bytes 786436
  229.8 26.1 %collective-permute-start.14 = (bf16[2,384,256]{1,2,0:T(8,128)(2,1)}, bf16[2,384,256]{1,2,0:T(8,128)(2,1)}, u32[]{:S(2)}, u32[]{:S(2)}) collective-permute-start(bf16[2,384,256]{1,2,0:T(8,128)(2,1)} %get-tuple-element.401), channel_id=1, source_target_pairs={{64,0},{72,8},{80,16},{88,24},{96,32},{104,40},{112,48},{120,56},{... | collective-permute-start | bytes 1179656 | tf_op jit(solution)/shard_map/ppermute | solution.py:18
  232.6 293.9 %collective-permute-start.13 = (bf16[2,384,256]{1,2,0:T(8,128)(2,1)}, bf16[2,384,256]{1,2,0:T(8,128)(2,1)S(1)}, u32[]{:S(2)}, u32[]{:S(2)}) collective-permute-start(bf16[2,384,256]{1,2,0:T(8,128)(2,1)} %get-tuple-element.402), channel_id=1, source_target_pairs={{56,0},{64,8},{72,16},{80,24},{88,32},{96,40},{104,48},{112,56},{1... | collective-permute-start | bytes 1179656 | tf_op jit(solution)/shard_map/ppermute | solution.py:18
  236.3 290.3 %collective-permute-start.12 = (bf16[2,384,256]{1,2,0:T(8,128)(2,1)}, bf16[2,384,256]{1,2,0:T(8,128)(2,1)S(1)}, u32[]{:S(2)}, u32[]{:S(2)}) collective-permute-start(bf16[2,384,256]{1,2,0:T(8,128)(2,1)} %get-tuple-element.403), channel_id=1, source_target_pairs={{8,0},{16,8},{24,16},{32,24},{40,32},{48,40},{56,48},{64,56},{72,6... | collective-permute-start | bytes 1179656 | tf_op jit(solution)/shard_map/ppermute | solution.py:18
  246.2 280.3 %collective-permute-start.11 = (bf16[2,384,256]{1,2,0:T(8,128)(2,1)}, bf16[2,384,256]{1,2,0:T(8,128)(2,1)S(1)}, u32[]{:S(2)}, u32[]{:S(2)}) collective-permute-start(bf16[2,384,256]{1,2,0:T(8,128)(2,1)} %get-tuple-element.404), channel_id=1, source_target_pairs={{0,8},{8,16},{16,24},{24,32},{32,40},{40,48},{48,56},{56,64},{64,7... | collective-permute-start | bytes 1179656 | tf_op jit(solution)/shard_map/ppermute | solution.py:18
  248.1 278.4 %collective-permute-start.10 = (bf16[2,384,256]{1,2,0:T(8,128)(2,1)}, bf16[2,384,256]{1,2,0:T(8,128)(2,1)}, u32[]{:S(2)}, u32[]{:S(2)}) collective-permute-start(bf16[2,384,256]{1,2,0:T(8,128)(2,1)} %get-tuple-element.405), channel_id=1, source_target_pairs={{0,56},{8,64},{16,72},{24,80},{32,88},{40,96},{48,104},{56,112},{6... | collective-permute-start | bytes 1179656 | tf_op jit(solution)/shard_map/ppermute | solution.py:18
  255.9 270.7 %collective-permute-start.9 = (bf16[2,384,256]{1,2,0:T(8,128)(2,1)}, bf16[2,384,256]{1,2,0:T(8,128)(2,1)}, u32[]{:S(2)}, u32[]{:S(2)}) collective-permute-start(bf16[2,384,256]{1,2,0:T(8,128)(2,1)} %get-tuple-element.406), channel_id=1, source_target_pairs={{0,64},{8,72},{16,80},{24,88},{32,96},{40,104},{48,112},{56,120},{... | collective-permute-start | bytes 1179656 | tf_op jit(solution)/shard_map/ppermute | solution.py:18
  529.6 4.0 copy-start.7
  531.6 4.2 copy-start.3
  531.6 4.1 copy-start.19
  537.1 2.6 copy-start.21
  537.1 2.6 copy-start.22
  1609.8 11.0 copy-start.1
  (2 other events, 2.7 us)
Sparse Core Ops, SparseCore 0:
  52.4 83.1 all-gather.3
  156.4 1453.3 all-gather.5
